TPU v7x, 32 devices: a whole 2x2x4 slice. The times are simulated.
32 devices in a mesh: ctx: 8 (over y, x, core), head: 4 (over z).
Axes of the slice: x: 2, y: 2, z: 4, core: 2. Of those that a mesh axis runs over, the one named last changes fastest.
Arguments:
- input_queries: bfloat16 [8192, 6144], P(('ctx', 'head')), may hold values from -6 to 6
- input_keys: bfloat16 [8192, 1024], P(('ctx', 'head')), may hold values from -6 to 6
- input_values: bfloat16 [8192, 1024], P(('ctx', 'head')), may hold values from -6 to 6
- cotangent: bfloat16 [8192, 6144], P(('ctx', 'head')), may hold values from -6 to 6
- block_list: int32 [16, 8], replicated, may hold values from 0 to 15, as said below
- block_count: int32 [16], replicated, may hold values from 1 to 8, as said below
Outputs:
- attn_out: bfloat16 [8192, 6144], P(('ctx', 'head'))
- grad_query: bfloat16 [8192, 6144], P(('ctx', 'head'))
- key_gradient: bfloat16 [8192, 1024], P(('ctx', 'head'))
- value_gradient: bfloat16 [8192, 1024], P(('ctx', 'head'))
Inputs may be any that keep to these rules, and one draw needn't show every extreme that they name: `block_list`: row b lists entry 0 = b itself, then distinct blocks of other ctx indices up to position block_count[b] - 1, block c belonging to ctx index c // 2; entries from position block_count[b] on repeat b and are unused. The rows of the 2 query blocks of one ctx index together name at most one block of any other ctx index. `block_count`: query block 0 lists 8 blocks.
All inputs are finite; a program needn't handle non-finite values.
Results may differ from a plain program's by a relative error of at most 0.015.
Values may be sent and summed in bfloat16 or wider, within the bound.
No kernel may reach another device: no remote copies, remote signals or barrier semaphores. Data moves between devices by JAX's collectives and lax.ppermute only.
A program may use at most 128 MiB of HBM per device.

v0:
```python
import jax
import jax.numpy as jnp
from jax import lax
from jax.sharding import PartitionSpec as P

QUERY_HEADS = 48
KEY_VALUE_HEADS = 8
HEAD_WIDTH = 128
BLOCK_TOKENS = 512


NEG_FILL = -1e30


def shards(input_queries, input_keys, input_values, cotangent, block_list, block_count):
    ctx_rank = lax.axis_index("ctx")
    query_loc, key_loc, value_loc, cot_loc = (
        lax.all_to_all(input_queries, "head", split_axis=1, concat_axis=0, tiled=True),
        lax.all_to_all(input_keys, "head", split_axis=1, concat_axis=0, tiled=True),
        lax.all_to_all(input_values, "head", split_axis=1, concat_axis=0, tiled=True),
        lax.all_to_all(cotangent, "head", split_axis=1, concat_axis=0, tiled=True),
    )
    tok_ctx = query_loc.shape[0]
    own_blocks = tok_ctx // BLOCK_TOKENS
    kv_local = key_loc.shape[1] // HEAD_WIDTH
    group_width = QUERY_HEADS // KEY_VALUE_HEADS
    half_width = kv_local * HEAD_WIDTH
    score_scale = HEAD_WIDTH ** (-0.5)
    own_table = jnp.concatenate([key_loc, value_loc], axis=1).reshape(
        own_blocks, BLOCK_TOKENS, 2 * half_width
    )
    blocked_queries = query_loc.reshape(own_blocks, BLOCK_TOKENS, kv_local, group_width, HEAD_WIDTH)
    cotangent_blocks = cot_loc.reshape(own_blocks, BLOCK_TOKENS, kv_local, group_width, HEAD_WIDTH)
    first_block = ctx_rank * own_blocks
    my_lists = lax.dynamic_slice_in_dim(block_list, first_block, own_blocks, 0)
    my_counts = lax.dynamic_slice_in_dim(block_count, first_block, own_blocks, 0)
    kv_table = lax.all_gather(own_table, "ctx", axis=0, tiled=True)

    def tile_parts(slot_id):
        tile_data = lax.dynamic_index_in_dim(kv_table, slot_id, 0, keepdims=False)
        tile_keys = tile_data[:, :half_width].reshape(BLOCK_TOKENS, kv_local, HEAD_WIDTH)
        tile_values = tile_data[:, half_width:].reshape(BLOCK_TOKENS, kv_local, HEAD_WIDTH)
        return (tile_keys, tile_values)

    def one_block(grad_table, inputs):
        query_b, cot_b, slot_ids, live_count = inputs
        stat_shape = (kv_local, group_width, BLOCK_TOKENS)

        def tile_scores(tile_keys):
            return (
                jnp.einsum("qgjd,kgd->gjqk", query_b, tile_keys, preferred_element_type=jnp.float32)
                * score_scale
            )

        def scan_stats(step_id, running):
            top_score, row_total = running
            tile_keys, tile_values = tile_parts(slot_ids[step_id])
            scores = tile_scores(tile_keys)
            new_top = jnp.maximum(top_score, jnp.max(scores, axis=-1))
            row_total = row_total * jnp.exp(top_score - new_top) + jnp.sum(
                jnp.exp(scores - new_top[..., None]), axis=-1
            )
            return (new_top, row_total)

        start_stats = (
            jnp.full(stat_shape, NEG_FILL, jnp.float32),
            jnp.zeros(stat_shape, jnp.float32),
        )
        top_score, row_total = lax.fori_loop(0, live_count, scan_stats, start_stats)
        log_total = top_score + jnp.log(row_total)

        def add_values(step_id, summed):
            tile_keys, tile_values = tile_parts(slot_ids[step_id])
            weights = jnp.exp(tile_scores(tile_keys) - log_total[..., None]).astype(jnp.bfloat16)
            return summed + jnp.einsum(
                "gjqk,kgd->qgjd", weights, tile_values, preferred_element_type=jnp.float32
            )

        out_shape = (BLOCK_TOKENS, kv_local, group_width, HEAD_WIDTH)
        attended = lax.fori_loop(
            0, live_count, add_values, jnp.zeros(out_shape, jnp.float32)
        ).astype(jnp.bfloat16)
        row_delta = jnp.sum(attended.astype(jnp.float32) * cot_b.astype(jnp.float32), axis=-1)
        row_delta = jnp.transpose(row_delta, (1, 2, 0))

        def add_grads(step_id, carried):
            grad_q, table_acc = carried
            slot_id = slot_ids[step_id]
            tile_keys, tile_values = tile_parts(slot_id)
            weights = jnp.exp(tile_scores(tile_keys) - log_total[..., None])
            weights_b = weights.astype(jnp.bfloat16)
            grad_weights = jnp.einsum(
                "qgjd,kgd->gjqk", cot_b, tile_values, preferred_element_type=jnp.float32
            )
            grad_scores = (weights * (grad_weights - row_delta[..., None])).astype(jnp.bfloat16)
            grad_q = grad_q + jnp.einsum(
                "gjqk,kgd->qgjd", grad_scores, tile_keys, preferred_element_type=jnp.float32
            )
            key_gradient_part = (
                jnp.einsum(
                    "gjqk,qgjd->kgd", grad_scores, query_b, preferred_element_type=jnp.float32
                )
                * score_scale
            )
            value_gradient_part = jnp.einsum(
                "gjqk,qgjd->kgd", weights_b, cot_b, preferred_element_type=jnp.float32
            )
            tile_grads = jnp.concatenate(
                [
                    key_gradient_part.reshape(BLOCK_TOKENS, half_width),
                    value_gradient_part.reshape(BLOCK_TOKENS, half_width),
                ],
                axis=1,
            )
            table_acc = table_acc.at[slot_id].add(tile_grads)
            return (grad_q, table_acc)

        grad_q, grad_table = lax.fori_loop(
            0, live_count, add_grads, (jnp.zeros(out_shape, jnp.float32), grad_table)
        )
        return (grad_table, (attended, (grad_q * score_scale).astype(jnp.bfloat16)))

    start_table = jnp.zeros((kv_table.shape[0], BLOCK_TOKENS, 2 * half_width), jnp.float32)
    grad_table, block_outs = lax.scan(
        one_block, start_table, (blocked_queries, cotangent_blocks, my_lists, my_counts)
    )
    own_grads = lax.psum_scatter(
        grad_table.astype(jnp.bfloat16), "ctx", scatter_dimension=0, tiled=True
    ).astype(jnp.float32)
    grad_key_loc = own_grads[:, :, :half_width].reshape(tok_ctx, half_width).astype(jnp.bfloat16)
    grad_value_loc = own_grads[:, :, half_width:].reshape(tok_ctx, half_width).astype(jnp.bfloat16)
    attn_loc = block_outs[0].reshape(tok_ctx, kv_local * group_width * HEAD_WIDTH)
    grad_query_loc = block_outs[1].reshape(tok_ctx, kv_local * group_width * HEAD_WIDTH)
    attn_out, grad_query, key_gradient, value_gradient = (
        lax.all_to_all(attn_loc, "head", split_axis=0, concat_axis=1, tiled=True),
        lax.all_to_all(grad_query_loc, "head", split_axis=0, concat_axis=1, tiled=True),
        lax.all_to_all(grad_key_loc, "head", split_axis=0, concat_axis=1, tiled=True),
        lax.all_to_all(grad_value_loc, "head", split_axis=0, concat_axis=1, tiled=True),
    )
    return (attn_out, grad_query, key_gradient, value_gradient)


def solution(mesh):
    placed = (
        P(("ctx", "head"), None),
        P(("ctx", "head"), None),
        P(("ctx", "head"), None),
        P(("ctx", "head"), None),
        P(),
        P(),
    )
    return jax.shard_map(
        shards,
        mesh=mesh,
        in_specs=placed,
        out_specs=(
            P(("ctx", "head"), None),
            P(("ctx", "head"), None),
            P(("ctx", "head"), None),
            P(("ctx", "head"), None),
        ),
        check_vma=False,
    )
```

profile of v0, /device:TPU:4, one launch (start us, length us, event | category | flops | bytes accessed | tf_op | source)
XLA Modules:
  0.0 1196.6 jit_solution(7652566791654043438)
XLA Ops:
  16.1 12.4 %all-to-all-done.1 = bf16[256,4,256]{0,2,1:T(8,128)(2,1)S(1)} async-done(((bf16[256,4,256]{0,2,1:T(8,128)(2,1)}), bf16[256,4,256]{0,2,1:T(8,128)(2,1)S(1)}, u32[]{:S(2)}, u32[]{:S(2)}) %all-to-all-start.1) | async-done | bytes 524320 | tf_op jit(solution)/shard_map/all_to_all | solution.py:19
  35.9 12.0 %all-to-all-done.2 = bf16[256,4,256]{0,2,1:T(8,128)(2,1)} async-done(((bf16[256,4,256]{0,2,1:T(8,128)(2,1)}), bf16[256,4,256]{0,2,1:T(8,128)(2,1)}, u32[]{:S(2)}, u32[]{:S(2)}) %all-to-all-start.2) | async-done | bytes 524320 | tf_op jit(solution)/shard_map/all_to_all | solution.py:20
  63.5 65.4 %all-to-all-done = bf16[256,4,1536]{0,2,1:T(8,128)(2,1)S(1)} async-done(((bf16[256,4,1536]{0,2,1:T(8,128)(2,1)}), bf16[256,4,1536]{0,2,1:T(8,128)(2,1)S(1)}, u32[]{:S(2)}, u32[]{:S(2)}) %all-to-all-start) | async-done | bytes 3145760 | tf_op jit(solution)/shard_map/all_to_all | solution.py:18
  134.1 13.1 %copy.115 = bf16[4,256,1536]{1,0,2:T(4,128)(2,1)} copy(bf16[4,256,1536]{1,2,0:T(8,128)(2,1)S(1)} %bitcast.245) | data formatting | bytes 6291456 | tf_op jit(solution)/shard_map/all_to_all | solution.py:18
  147.2 6.5 reshape.114
  156.0 48.1 %all-to-all-done.3 = bf16[256,4,1536]{0,2,1:T(8,128)(2,1)} async-done(((bf16[256,4,1536]{0,2,1:T(8,128)(2,1)}), bf16[256,4,1536]{0,2,1:T(8,128)(2,1)}, u32[]{:S(2)}, u32[]{:S(2)}) %all-to-all-start.3) | async-done | bytes 3145760 | tf_op jit(solution)/shard_map/all_to_all | solution.py:21
  216.8 12.3 %copy.123 = bf16[16,512,512]{1,2,0:T(8,128)(2,1)} copy(bf16[16,512,512]{2,1,0:T(8,128)(2,1)} %all-gather.2.cloned.1.call-done) | data formatting | bytes 16777216 | tf_op jit(solution)/shard_map/while | solution.py:124
  229.1 7.9 broadcast_in_dim.15
  237.0 803.5 %while.52 = (s32[]{:T(128)}, f32[16,512,512]{1,2,0:T(8,128)}, bf16[2,512,2,6,128]{1,4,3,2,0:T(8,128)(2,1)}, bf16[2,512,2,6,128]{1,4,3,2,0:T(8,128)(2,1)}, s32[2]...) while((s32[]{:T(128)}, f32[16,512,512]{1,2,0:T(8,128)}, ...), condition=%wide.region_11.12_spmd, body=%wide.region_0.11_spmd.sunk | while | flops 6501576704 | bytes 196652144 | solution.py:124
  250.5 68.9 %while.53 = (s32[]{:T(128)}, f32[2,6,512]{2,1,0:T(8,128)S(1)}, f32[2,6,512]{2,1,0:T(8,128)S(1)}, s32[]{:T(128)}, s32[8]{0:T(128)S(1)}, /*index=5*/bf16[16,512,51...) while((s32[]{:T(128)}, f32[2,6,512]{2,1,0:T(8,128)S(1)}, ...), condition=%wide.region_4.4_spmd, body=%wide.region_1.3_spmd.sunk | while | flops 821047296 | bytes 28893384 | solution.py:69
  321.6 92.1 %while.54 = (s32[]{:T(128)}, f32[512,2,6,128]{0,3,2,1:T(8,128)}, s32[]{:T(128)}, s32[8]{0:T(128)S(1)}, bf16[16,512,512]{1,2,0:T(8,128)(2,1)}, /*index=5*/bf16[51...) while((s32[]{:T(128)}, f32[512,2,6,128]{0,3,2,1:T(8,128)}, ...), condition=%wide.region_6.6_spmd, body=%wide.region_5.5_spmd.sunk | while | flops 1620836352 | bytes 10510537 | solution.py:80
  326.6 6.4 bitcast_add_fusion.4
  338.0 6.4 bitcast_add_fusion.4
  418.5 220.2 %while.55 = (s32[]{:T(128)}, f32[512,2,6,128]{0,3,2,1:T(8,128)}, f32[16,512,512]{1,2,0:T(8,128)}, s32[]{:T(128)}, s32[8]{0:T(128)S(1)}, /*index=5*/bf16[16,512,5...) while((s32[]{:T(128)}, f32[512,2,6,128]{0,3,2,1:T(8,128)}, ...), condition=%wide.region_10.10_spmd, body=%wide.region_8.9_spmd.sunk | while | flops 4053401600 | bytes 128787832 | solution.py:118
  647.1 68.9 %while.53 = (s32[]{:T(128)}, f32[2,6,512]{2,1,0:T(8,128)S(1)}, f32[2,6,512]{2,1,0:T(8,128)S(1)}, s32[]{:T(128)}, s32[8]{0:T(128)S(1)}, /*index=5*/bf16[16,512,51...) while((s32[]{:T(128)}, f32[2,6,512]{2,1,0:T(8,128)S(1)}, ...), condition=%wide.region_4.4_spmd, body=%wide.region_1.3_spmd.sunk | while | flops 821047296 | bytes 28893384 | solution.py:69
  718.1 92.1 %while.54 = (s32[]{:T(128)}, f32[512,2,6,128]{0,3,2,1:T(8,128)}, s32[]{:T(128)}, s32[8]{0:T(128)S(1)}, bf16[16,512,512]{1,2,0:T(8,128)(2,1)}, /*index=5*/bf16[51...) while((s32[]{:T(128)}, f32[512,2,6,128]{0,3,2,1:T(8,128)}, ...), condition=%wide.region_6.6_spmd, body=%wide.region_5.5_spmd.sunk | while | flops 1620836352 | bytes 10510537 | solution.py:80
  815.1 220.1 %while.55 = (s32[]{:T(128)}, f32[512,2,6,128]{0,3,2,1:T(8,128)}, f32[16,512,512]{1,2,0:T(8,128)}, s32[]{:T(128)}, s32[8]{0:T(128)S(1)}, /*index=5*/bf16[16,512,5...) while((s32[]{:T(128)}, f32[512,2,6,128]{0,3,2,1:T(8,128)}, ...), condition=%wide.region_10.10_spmd, body=%wide.region_8.9_spmd.sunk | while | flops 4053401600 | bytes 128787832 | solution.py:118
  1040.5 13.9 %copy.129 = bf16[16,512,512]{2,1,0:T(8,128)(2,1)} copy(f32[16,512,512]{1,2,0:T(8,128)} %get-tuple-element.903) | data formatting | bytes 25165824 | tf_op jit(solution)/shard_map/while | solution.py:124
  1071.1 6.8 copy.125
  1077.9 8.7 all_to_all.112
  1090.8 18.6 %all-to-all-done.5 = bf16[4,256,1536]{1,2,0:T(8,128)(2,1)S(1)} async-done(((bf16[4,256,1536]{1,2,0:T(8,128)(2,1)}), bf16[4,256,1536]{1,2,0:T(8,128)(2,1)S(1)}, u32[]{:S(2)}, u32[]{:S(2)}) %all-to-all-start.5) | async-done | bytes 3145760 | tf_op jit(solution)/shard_map/all_to_all | solution.py:136
  1114.1 10.2 reduce-scatter.2.cloned.1.call-done
  1126.6 31.6 %all-to-all-done.4 = bf16[4,256,1536]{1,2,0:T(8,128)(2,1)} async-done(((bf16[4,256,1536]{1,2,0:T(8,128)(2,1)}), bf16[4,256,1536]{1,2,0:T(8,128)(2,1)}, u32[]{:S(2)}, u32[]{:S(2)}) %all-to-all-start.4) | async-done | bytes 3145760 | tf_op jit(solution)/shard_map/all_to_all | solution.py:135
  1158.2 14.5 %all_to_all.134 = bf16[4,256,256]{2,1,0:T(8,128)(2,1)} all-to-all(bf16[4,256,256]{2,1,0:T(8,128)(2,1)} %bitcast.256), channel_id=1, replica_groups=mesh['ctx'=8,'head'=4] {'head'}, dimensions={0} | all-to-all | bytes 1048576 | tf_op jit(solution)/shard_map/all_to_all | solution.py:137
  (570 shorter events, 744.4 us)
Async XLA Ops:
  7.2 126.8 %copy-start = (s32[16,8]{0,1:T(8,128)S(1)}, s32[16,8]{0,1:T(8,128)}, u32[]{:S(2)}) copy-start(s32[16,8]{0,1:T(8,128)} %param.20) | copy-start | bytes 1540
  9.2 19.4 %all-to-all-start.1 = ((bf16[256,4,256]{0,2,1:T(8,128)(2,1)}), bf16[256,4,256]{0,2,1:T(8,128)(2,1)S(1)}, u32[]{:S(2)}, u32[]{:S(2)}) async-start(bf16[256,4,256]{0,2,1:T(8,128)(2,1)} %bitcast.44), calls=%async_computation.1 | async-start | bytes 1048576 | tf_op jit(solution)/shard_map/all_to_all | solution.py:19
  29.4 22.8 %copy-start.6 = (bf16[256,6144]{1,0:T(8,128)(2,1)S(1)}, bf16[256,6144]{1,0:T(8,128)(2,1)}, u32[]{:S(2)}) copy-start(bf16[256,6144]{1,0:T(8,128)(2,1)} %param.16) | copy-start | bytes 9437188
  29.4 18.5 %all-to-all-start.2 = ((bf16[256,4,256]{0,2,1:T(8,128)(2,1)}), bf16[256,4,256]{0,2,1:T(8,128)(2,1)}, u32[]{:S(2)}, u32[]{:S(2)}) async-start(bf16[256,4,256]{0,2,1:T(8,128)(2,1)} %bitcast.250), calls=%async_computation.2 | async-start | bytes 1048576 | tf_op jit(solution)/shard_map/all_to_all | solution.py:20
  33.8 183.0 %all-gather.2.cloned.1.call-start = ((), (), s32[]{:S(2)}) async-start(), calls=%async_computation.9 | async-start | bytes 9437184 | tf_op jit(solution)/shard_map/all_gather | solution.py:37
  55.0 73.9 %all-to-all-start = ((bf16[256,4,1536]{0,2,1:T(8,128)(2,1)}), bf16[256,4,1536]{0,2,1:T(8,128)(2,1)S(1)}, u32[]{:S(2)}, u32[]{:S(2)}) async-start(bf16[256,4,1536]{0,2,1:T(8,128)(2,1)} %bitcast.248), calls=%async_computation | async-start | bytes 6291456 | tf_op jit(solution)/shard_map/all_to_all | solution.py:18
  128.9 75.2 %all-to-all-start.3 = ((bf16[256,4,1536]{0,2,1:T(8,128)(2,1)}), bf16[256,4,1536]{0,2,1:T(8,128)(2,1)}, u32[]{:S(2)}, u32[]{:S(2)}) async-start(bf16[256,4,1536]{0,2,1:T(8,128)(2,1)} %bitcast.246), calls=%async_computation.3 | async-start | bytes 6291456 | tf_op jit(solution)/shard_map/all_to_all | solution.py:21
  133.8 990.6 %reduce-scatter.2.cloned.1.call-start = ((), (), s32[]{:S(2)}) async-start(), calls=%async_computation.10 | async-start | bytes 9437184 | tf_op jit(solution)/shard_map/reduce_scatter | solution.py:127
  429.5 11.3 copy-start.3
  457.0 11.3 copy-start.3
  484.4 11.3 copy-start.3
  511.8 11.3 copy-start.3
  566.7 11.3 copy-start.3
  594.1 11.3 copy-start.3
  621.6 11.3 copy-start.3
  826.1 11.3 copy-start.3
  853.5 11.3 copy-start.3
  908.5 11.3 copy-start.3
  935.9 11.3 copy-start.3
  963.4 11.3 copy-start.3
  1018.2 11.3 copy-start.3
  1067.4 42.1 %all-to-all-start.5 = ((bf16[4,256,1536]{1,2,0:T(8,128)(2,1)}), bf16[4,256,1536]{1,2,0:T(8,128)(2,1)S(1)}, u32[]{:S(2)}, u32[]{:S(2)}) async-start(bf16[4,256,1536]{1,2,0:T(8,128)(2,1)} %copy.128), calls=%async_computation.5 | async-start | bytes 6291456 | tf_op jit(solution)/shard_map/all_to_all | solution.py:136
  1109.5 48.7 %all-to-all-start.4 = ((bf16[4,256,1536]{1,2,0:T(8,128)(2,1)}), bf16[4,256,1536]{1,2,0:T(8,128)(2,1)}, u32[]{:S(2)}, u32[]{:S(2)}) async-start(bf16[4,256,1536]{1,2,0:T(8,128)(2,1)} %copy.126), calls=%async_computation.4 | async-start | bytes 6291456 | tf_op jit(solution)/shard_map/all_to_all | solution.py:135
  1172.7 14.5 %all-to-all-start.7 = ((bf16[4,256,256]{2,1,0:T(8,128)(2,1)}), bf16[4,256,256]{2,1,0:T(8,128)(2,1)}, u32[]{:S(2)}, u32[]{:S(2)}) async-start(bf16[4,256,256]{2,1,0:T(8,128)(2,1)} %bitcast.254), calls=%async_computation.8 | async-start | bytes 1048576 | tf_op jit(solution)/shard_map/all_to_all | solution.py:138
  (64 other events, 258.9 us)
Sparse Core Ops, SparseCore 0:
  52.3 52.9 all-gather.1
  1054.6 69.6 reduce-scatter.1
where the time goes:
time: 1210 us; the launch traced here: 1200 us
  matrix products  423 us (35%)
  local copies, waits for them, and re-layouts  251 us (21%)
  waiting for transfers between devices  200 us (17%)
  loops' own time  143 us (12%)
  other arithmetic  121 us (10%)
  starting transfers between devices  30.5 us (3%)
  between operations  14.6 us (1%)
  blocking collectives  14.5 us (1%)
    dot_general x16, matrix products, add_values(): jnp.einsum('gjqk,kgd->qgjd', weights, tile_values, preferred_element_type...  103 us
    dot_general x16, matrix products, add_grads(): jnp.einsum('qgjd,kgd->gjqk', cot_b, tile_values, preferred_element_type=j...  99.4 us
    dot_general x16, matrix products, add_grads(): jnp.einsum('gjqk,qgjd->kgd', grad_scores, query_b, preferred_element_type...  81 us
    all_to_all x1, waiting for transfers between devices, shards(): lax.all_to_all(input_queries, 'head', split_axis=1, concat_axis=0, tiled=...  65.4 us
    dot_general x32, matrix products, tile_scores(): jnp.einsum('qgjd,kgd->gjqk', query_b, tile_keys, preferred_element_type=j...  59.3 us
    scatter-add x16, other arithmetic, add_grads(): table_acc = table_acc.at[slot_id].add(tile_grads)  55.5 us
    dot_general x16, matrix products, add_grads(): jnp.einsum('gjqk,qgjd->kgd', weights_b, cot_b, preferred_element_type=jnp...  54.1 us
    squeeze x48, local copies, waits for them, and re-layouts, tile_parts(): tile_data = lax.dynamic_index_in_dim(kv_table, slot_id, 0, keepdims=False)  51.8 us
  transfers between devices with their start and end apart: 9, of which 8 were waited for; matrix products, arithmetic and copies ran while one was open for 7% of the time, Pallas kernels for 0%

commit v1 on v0

v1 whole, which is shorter than its diff:
```python
import functools
import math

import jax
import jax.numpy as jnp
from jax import lax
from jax.experimental import pallas as pl
from jax.experimental.pallas import tpu as pltpu
from jax.sharding import PartitionSpec as P


QUERY_HEADS = 48
KEY_VALUE_HEADS = 8
HEAD_WIDTH = 128
BLOCK_TOKENS = 512
GROUP_WIDTH = QUERY_HEADS // KEY_VALUE_HEADS

SCORE_SCALE = HEAD_WIDTH ** (-0.5)
EXP2_SCALE = SCORE_SCALE * math.log2(math.e)
LOWEST = -3.0e38
VMEM_BYTES = 62 * 1024 * 1024


NT = (((1,), (1,)), ((), ()))
NN = (((1,), (0,)), ((), ()))
TN = (((0,), (0,)), ((), ()))


def dot(a, b, dims):
    return lax.dot_general(a, b, dims, preferred_element_type=jnp.float32)


def bf16(*shape):
    return jax.ShapeDtypeStruct(shape, jnp.bfloat16)


ANY = pl.BlockSpec(memory_space=pl.ANY)
VMEM = pl.BlockSpec(memory_space=pltpu.VMEM)
SMEM = pl.BlockSpec(memory_space=pltpu.SMEM)


class Copies:
    def __init__(self, sems):
        self.sems, self.made = sems, 0

    def make(self, src, dst):
        self.made += 1
        return pltpu.make_async_copy(src, dst, self.sems.at[self.made - 1])

    @staticmethod
    def run(copies):
        for copy in copies:
            copy.start()
        for copy in copies:
            copy.wait()


class Layout:
    def __init__(self, ctx_size, head_size, tokens):
        self.group = KEY_VALUE_HEADS
        assert ctx_size % self.group == 0
        self.ctx_size, self.heads, self.tokens = ctx_size, head_size, tokens
        self.line = ctx_size // self.group * head_size
        self.per_ctx = tokens * head_size // BLOCK_TOKENS
        self.per_block = BLOCK_TOKENS // tokens
        self.blocks = ctx_size * self.per_ctx
        self.others = range(1, self.group)

    def device(self, w, u):
        m, h = divmod(w, self.heads)
        return (m * self.group + u) * self.heads + h

    def swap(self, value, x):
        pairs = [
            (self.device(w, u), self.device(w, u ^ x))
            for w in range(self.line)
            for u in range(self.group)
        ]
        return lax.ppermute(value, ("ctx", "head"), pairs)

    def shift(self, value, sources, step):
        pairs = [
            (self.device(w, u), self.device(w + step, u)) for w in sources for u in range(self.group)
        ]
        return lax.ppermute(value, ("ctx", "head"), pairs)

    def place(self, w):
        m, h = w // self.heads, w % self.heads
        first = (m * self.per_ctx + h // self.per_block) * self.group
        return first, pl.multiple_of(h % self.per_block * self.tokens, self.tokens)

    def table_block(self, block, u):
        ctx = block // self.per_ctx
        first = (ctx // self.group * self.per_ctx + block % self.per_ctx) * self.group
        return first + jnp.bitwise_xor(ctx % self.group, u)


def copy_call(body, ins, specs, outs, n, out_spec=ANY):
    def kernel(*refs):
        sems = refs[-1]
        Copies.run(list(body(Copies(sems), refs[: len(ins)], refs[len(ins) : -1])))

    moved = 4 * sum(math.prod(o.shape) for o in outs)
    return pl.pallas_call(
        kernel,
        out_shape=outs,
        in_specs=specs,
        out_specs=[out_spec] * len(outs),
        scratch_shapes=[pltpu.SemaphoreType.DMA((n,))],
        compiler_params=pltpu.CompilerParams(vmem_limit_bytes=VMEM_BYTES),
        cost_estimate=pl.CostEstimate(flops=0, transcendentals=0, bytes_accessed=moved),
    )(*ins)


def columns(index, count=1):
    return pl.ds(pl.multiple_of(index * HEAD_WIDTH, HEAD_WIDTH), count * HEAD_WIDTH)


def pack(lay, u, arrays, count, places):
    def body(copies, ins, outs):
        rank, *raw = ins
        for x, out in zip(places, outs, strict=True):
            cols = columns(jnp.bitwise_xor(rank[0], x) * count, count)
            for half in range(2):
                yield copies.make(raw[half].at[:, cols], out.at[half])

    outs = [bf16(2, lay.tokens, count * HEAD_WIDTH)] * len(places)
    return copy_call(body, [u, *arrays], [SMEM, VMEM, VMEM], outs, 2 * len(places))


def unpack(lay, u, slabs, count):
    def body(copies, ins, outs):
        rank, *parts = ins
        for x, part in enumerate(parts):
            cols = columns(jnp.bitwise_xor(rank[0], x) * count, count)
            for half in range(2):
                yield copies.make(part.at[half], outs[half].at[:, cols])

    outs = [bf16(lay.tokens, lay.group * count * HEAD_WIDTH)] * 2
    specs = [SMEM] + [ANY] * lay.group
    return copy_call(body, [u, *slabs], specs, outs, 2 * lay.group, VMEM)


def collect(lay, slabs):
    def body(copies, ins, outs):
        for x, part in enumerate(ins):
            for half in range(2):
                yield copies.make(part.at[half], outs[0].at[half, x])

    outs = [bf16(2, lay.group, lay.tokens, HEAD_WIDTH)]
    specs = [ANY] * lay.group
    return copy_call(body, list(slabs), specs, outs, 2 * lay.group, VMEM)[0]


def split(lay, terms):
    def kernel(*refs):
        ins, outs = refs[: len(terms)], refs[len(terms) :]
        for x, out in enumerate(outs):
            for half in range(2):
                total = ins[0][half, x].astype(jnp.float32)
                for term in ins[1:]:
                    total += term[half, x].astype(jnp.float32)
                out[half] = total.astype(jnp.bfloat16)

    outs = [bf16(2, lay.tokens, HEAD_WIDTH)] * lay.group
    moved = 2 * (len(terms) + 1) * math.prod(terms[0].shape)
    return pl.pallas_call(
        kernel,
        out_shape=outs,
        in_specs=[VMEM] * len(terms),
        out_specs=[VMEM] * len(outs),
        cost_estimate=pl.CostEstimate(flops=0, transcendentals=0, bytes_accessed=moved),
        name="split",
    )(*terms)


def attention_kernel(lay, list_ref, count_ref, where_ref, *refs):
    refs = list(refs)

    def take(n):
        taken = refs[:n]
        del refs[:n]
        return taken

    raw, slabs = take(2), take(lay.group - 1)
    own_table, below, above = take(1)[0], take(lay.line - 1), take(lay.line - 1)
    outs, own_sums, to_below, to_above = take(lay.group), take(1)[0], take(lay.line - 1), take(lay.line - 1)
    q_scr, do_scr, k_tab, v_tab, dk_acc, dv_acc, s_scr, e_scr, m_scr, o_acc, gq_acc, o_scr, sems = refs
    u, w = where_ref[0], where_ref[1]
    heads, rows = GROUP_WIDTH, lay.tokens
    made = Copies(sems)

    def table_copies(plane, table):
        first, row = lay.place(plane)
        dst = pl.ds(first, lay.group), pl.ds(row, rows)
        return [made.make(table.at[0], k_tab.at[dst]), made.make(table.at[1], v_tab.at[dst])]

    copies = []
    for x in range(lay.group):
        for half, dst in enumerate((q_scr, do_scr)):
            if x == 0:
                src = raw[half].at[:, columns(u * heads, heads)]
            else:
                src = slabs[x - 1].at[half]
            copies.append(made.make(src, dst.at[x]))
    copies += table_copies(w, own_table)
    guarded = []
    for k in range(1, lay.line):
        guarded.append((w >= k, table_copies(w - k, below[k - 1])))
        guarded.append((w + k < lay.line, table_copies(w + k, above[k - 1])))
    for copy in copies:
        copy.start()
    for valid, some in guarded:

        @pl.when(valid)
        def _():
            for copy in some:
                copy.start()

    dk_acc[...] = jnp.zeros_like(dk_acc)
    dv_acc[...] = jnp.zeros_like(dv_acc)
    for copy in copies:
        copy.wait()
    for valid, some in guarded:

        @pl.when(valid)
        def _():
            for copy in some:
                copy.wait()

    repeat = BLOCK_TOKENS // HEAD_WIDTH

    def widen(x):
        return jnp.concatenate([x] * repeat, axis=1)

    cols = [pl.ds(g * HEAD_WIDTH, HEAD_WIDTH) for g in range(heads)]
    results = [
        [made.make(src.at[x], outs[x].at[half]) for half, src in enumerate((do_scr, q_scr))]
        for x in range(lay.group)
    ]
    plane_block = w // lay.heads * lay.group * lay.per_ctx + w % lay.heads // lay.per_block

    def one(x, carry):
        mine = plane_block + jnp.bitwise_xor(u, x) * lay.per_ctx
        live = count_ref[mine]
        m_scr[...] = jnp.full_like(m_scr, LOWEST)

        def scores(i, c):
            block = lay.table_block(list_ref[mine, i], u)
            for g in range(heads):
                s = dot(q_scr[x, :, cols[g]], k_tab[block], NT)
                s_scr[i, g] = s
                m = m_scr[g]
                for part in range(repeat):
                    m = jnp.maximum(m, s[:, part * HEAD_WIDTH : (part + 1) * HEAD_WIDTH])
                m_scr[g] = m
            return c

        lax.fori_loop(0, live, scores, 0)
        for g in range(heads):
            top = jnp.max(m_scr[g], axis=1, keepdims=True)
            m_scr[g] = jnp.broadcast_to(top, m_scr.shape[1:])
        o_acc[...] = jnp.zeros_like(o_acc)

        def weigh(i, c):
            block = lay.table_block(list_ref[mine, i], u)
            ones = jnp.ones((BLOCK_TOKENS, HEAD_WIDTH), jnp.bfloat16)
            v_ones = jnp.concatenate([v_tab[block], ones], axis=1)
            for g in range(heads):
                e = jnp.exp2((s_scr[i, g] - widen(m_scr[g])) * EXP2_SCALE)
                e = e.astype(jnp.bfloat16)
                e_scr[i, g] = e
                o_acc[g] += dot(e, v_ones, NN)
            return c

        lax.fori_loop(0, live, weigh, 0)
        for g in range(heads):
            inverse = 1.0 / o_acc[g, :, HEAD_WIDTH:]
            attended = (o_acc[g, :, :HEAD_WIDTH] * inverse).astype(jnp.bfloat16)
            o_scr[:, cols[g]] = attended
            cot = do_scr[x, :, cols[g]].astype(jnp.float32)
            delta = jnp.sum(attended.astype(jnp.float32) * cot, axis=1, keepdims=True)
            m_scr[g] = delta * inverse
            do_scr[x, :, cols[g]] = (cot * inverse).astype(jnp.bfloat16)
        gq_acc[...] = jnp.zeros_like(gq_acc)

        def grads(i, c):
            block = lay.table_block(list_ref[mine, i], u)
            dk, dv = None, None
            for g in range(heads):
                cot_n = do_scr[x, :, cols[g]]
                e = e_scr[i, g]
                dp = dot(cot_n, v_tab[block], NT)
                ds = e * (dp - widen(m_scr[g])).astype(jnp.bfloat16)
                gq_acc[g] += dot(ds, k_tab[block], NN)
                dk_g = dot(ds, q_scr[x, :, cols[g]], TN)
                dv_g = dot(e, cot_n, TN)
                dk = dk_g if dk is None else dk + dk_g
                dv = dv_g if dv is None else dv + dv_g
            dk_acc[block] += dk
            dv_acc[block] += dv
            return c

        lax.fori_loop(0, live, grads, 0)
        for g in range(heads):
            q_scr[x, :, cols[g]] = (gq_acc[g] * SCORE_SCALE).astype(jnp.bfloat16)
        do_scr[x] = o_scr[...]
        for place in range(lay.group):

            @pl.when(x == place)
            def _():
                for copy in results[place]:
                    copy.start()

        return carry

    lax.fori_loop(0, lay.group, one, 0)

    def narrow(b, carry):
        k_tab[b] = (dk_acc[b] * SCORE_SCALE).astype(jnp.bfloat16)
        v_tab[b] = dv_acc[b].astype(jnp.bfloat16)
        return carry

    lax.fori_loop(0, lay.blocks, narrow, 0)

    def sum_copies(plane, out):
        first, row = lay.place(plane)
        src = pl.ds(first, lay.group), pl.ds(row, rows)
        return [made.make(k_tab.at[src], out.at[0]), made.make(v_tab.at[src], out.at[1])]

    copies = sum_copies(w, own_sums)
    guarded = []
    for k in range(1, lay.line):
        guarded.append((w >= k, sum_copies(w - k, to_below[k - 1])))
        guarded.append((w + k < lay.line, sum_copies(w + k, to_above[k - 1])))
    for copy in copies:
        copy.start()
    for valid, some in guarded:

        @pl.when(valid)
        def _():
            for copy in some:
                copy.start()

    for valid, some in guarded:

        @pl.when(valid)
        def _():
            for copy in some:
                copy.wait()

    for copy in copies + [c for some in results for c in some]:
        copy.wait()


def attention(lay, lists, counts, where, raw, slabs, own_table, below, above):
    bf, f32 = jnp.bfloat16, jnp.float32
    width = GROUP_WIDTH * HEAD_WIDTH
    whole = (lay.blocks, BLOCK_TOKENS, HEAD_WIDTH)
    own = (lay.group, lay.tokens, width)
    most = lists.shape[1]
    tile = (GROUP_WIDTH, lay.tokens, BLOCK_TOKENS)
    far = 2 * (lay.line - 1)
    scratch = [
        *[pltpu.VMEM(own, bf)] * 2,
        *[pltpu.VMEM(whole, bf)] * 2,
        *[pltpu.VMEM(whole, f32)] * 2,
        pltpu.VMEM((most, *tile), f32),
        pltpu.VMEM((most, *tile), bf),
        pltpu.VMEM((GROUP_WIDTH, lay.tokens, HEAD_WIDTH), f32),
        pltpu.VMEM((GROUP_WIDTH, lay.tokens, 2 * HEAD_WIDTH), f32),
        pltpu.VMEM((GROUP_WIDTH, lay.tokens, HEAD_WIDTH), f32),
        pltpu.VMEM((lay.tokens, width), bf),
        pltpu.SemaphoreType.DMA((4 * lay.group + 4 * far + 4,)),
    ]
    table = (2, lay.group, lay.tokens, HEAD_WIDTH)
    out_shape = [bf16(2, lay.tokens, width)] * lay.group + [bf16(*table)] * (1 + far)
    operands = [*raw, *slabs, own_table, *below, *above]
    tiles = lay.group * most // 2
    return pl.pallas_call(
        functools.partial(attention_kernel, lay),
        out_shape=out_shape,
        grid_spec=pltpu.PrefetchScalarGridSpec(
            num_scalar_prefetch=3,
            grid=(1,),
            in_specs=[ANY] * len(operands),
            out_specs=[ANY] * len(out_shape),
            scratch_shapes=scratch,
        ),
        compiler_params=pltpu.CompilerParams(vmem_limit_bytes=VMEM_BYTES),
        cost_estimate=pl.CostEstimate(
            flops=tiles * 24 * math.prod(tile) * HEAD_WIDTH,
            transcendentals=tiles * math.prod(tile),
            bytes_accessed=32 * 1024 * 1024,
        ),
        name="attention",
    )(lists, counts, where, *operands)


def add(a, b):
    return (a.astype(jnp.float32) + b.astype(jnp.float32)).astype(jnp.bfloat16)


def shards(ctx_size, head_size, queries, keys, values, cotangent, block_list, block_count):
    lay = Layout(ctx_size, head_size, queries.shape[0])
    ctx_rank, head_rank = lax.axis_index("ctx"), lax.axis_index("head")
    u = lax.rem(ctx_rank, lay.group)
    w = ctx_rank // lay.group * lay.heads + head_rank
    where = jnp.stack([u, w]).astype(jnp.int32)
    n = lay.line

    local, *sent = pack(lay, where, (keys, values), 1, range(lay.group))
    came = [lay.swap(s, x) for x, s in zip(lay.others, sent)]
    own_table = collect(lay, [local, *came])
    below, above = [own_table], [own_table]
    for k in range(1, n):
        below.append(lay.shift(below[-1], range(k - 1, n - 1), 1))
        above.append(lay.shift(above[-1], range(1, n - k + 1), -1))
    sent = pack(lay, where, (queries, cotangent), GROUP_WIDTH, lay.others)
    slabs = [lay.swap(s, x) for x, s in zip(lay.others, sent)]
    outs = attention(
        lay,
        block_list,
        block_count,
        where,
        (queries, cotangent),
        slabs,
        own_table,
        below[1:],
        above[1:],
    )
    slabs, outs = outs[: lay.group], outs[lay.group :]
    own_sums, to_below, to_above = outs[0], outs[1:n], outs[n:]
    up, down = to_above[n - 2], to_below[n - 2]
    for k in range(n - 1, 0, -1):
        up = lay.shift(up, range(0, n - k), 1)
        down = lay.shift(down, range(k, n), -1)
        if k > 1:
            up, down = add(up, to_above[k - 2]), add(down, to_below[k - 2])
    local, *sent = split(lay, [own_sums, up, down])
    came = [lay.swap(s, x) for x, s in zip(lay.others, sent)]
    key_grad, value_grad = unpack(lay, where, [local, *came], 1)
    came = [lay.swap(s, x) for x, s in zip(lay.others, slabs[1:])]
    attn_out, grad_query = unpack(lay, where, [slabs[0], *came], GROUP_WIDTH)
    return attn_out, grad_query, key_grad, value_grad


def solution(mesh):
    placed = P(("ctx", "head"), None)

    def body(*args):
        return shards(mesh.shape["ctx"], mesh.shape["head"], *args)

    return jax.shard_map(
        body,
        mesh=mesh,
        in_specs=(placed,) * 4 + (P(), P()),
        out_specs=(placed,) * 4,
        check_vma=False,
    )
```

time: 1210 us -> 415 us (0.34)
  the two profiles are of different devices: /device:TPU:4 before, /device:TPU:25 now
where the time goes in v1:
time: 415 us
  waiting for transfers between devices  198 us (48%)
  Pallas kernels  149 us (36%)
  starting transfers between devices  60.6 us (15%)
    pallas_call x1, Pallas kernels, attention(): pl.pallas_call(functools.partial(attention_kernel, lay), out_shape=out_sh...  127 us
    ppermute x28, waiting for transfers between devices, swap(): return lax.ppermute(value, ('ctx', 'head'), pairs)  122 us
    ppermute x12, waiting for transfers between devices, shift(): return lax.ppermute(value, ('ctx', 'head'), pairs)  76.7 us
    ppermute x28, starting transfers between devices, swap(): return lax.ppermute(value, ('ctx', 'head'), pairs)  35.4 us
    ppermute x12, starting transfers between devices, shift(): return lax.ppermute(value, ('ctx', 'head'), pairs)  25.1 us
    pallas_call x5, Pallas kernels, copy_call(): pl.pallas_call(kernel, out_shape=outs, in_specs=specs, out_specs=[out_spe...  19.4 us
  transfers between devices with their start and end apart: 40, of which 15 were waited for; matrix products, arithmetic and copies ran while one was open for 1% of the time, Pallas kernels for 4%

profile of v1, /device:TPU:25, one launch (start us, length us, event | category | flops | bytes accessed | tf_op | source)
XLA Modules:
  0.0 414.6 jit_solution(12483654751682586018)
XLA Ops:
  10.0 3.0 collective-permute-start.13
  13.4 6.5 %collective-permute-done.11.refs_5_ = bf16[2,256,128]{2,1,0:T(8,128)(2,1)S(1)} collective-permute-done((bf16[2,256,128]{2,1,0:T(8,128)(2,1)}, bf16[2,256,128]{2,1,0:T(8,128)(2,1)S(1)}, u32[]{:S(2)}, u32[]{:S(2)}) %collective-permute-start.11) | collective-permute-done | bytes 131104 | tf_op jit(solution)/shard_map/ppermute | solution.py:79
  26.4 5.4 %shard_map.93 = (bf16[2,256,768]{2,1,0:T(8,128)(2,1)}, bf16[2,256,768]{2,1,0:T(8,128)(2,1)}, bf16[2,256,768]{2,1,0:T(8,128)(2,1)}, bf16[2,256,768]{2,1,0:T(8,128...) custom-call(s32[2]{0:T(128)} %pad_add_fusion.refs_0_.where_ref, ...), custom_call_target="tpu_custom_call" | custom-call | bytes 11010048 | tf_op jit(solution)/shard_map/pallas_call | solution.py:104
  32.3 15.5 %collective-permute-done.17.refs_13_ = bf16[2,8,256,128]{3,2,1,0:T(8,128)(2,1)S(1)} collective-permute-done((bf16[2,8,256,128]{3,2,1,0:T(8,128)(2,1)}, bf16[2,8,256,128]{3,2,1,0:T(8,128)(2,1)S(1)}, u32[]{:S(2)}, u32[]{:S(2)}) %collective-permute-start.17) | collective-permute-done | bytes 1048608 | tf_op jit(solution)/shard_map/ppermute | solution.py:85
  48.5 3.2 collective-permute-done.14.refs_10_
  58.8 18.6 %collective-permute-done.15.refs_11_ = bf16[2,8,256,128]{3,2,1,0:T(8,128)(2,1)} collective-permute-done((bf16[2,8,256,128]{3,2,1,0:T(8,128)(2,1)}, bf16[2,8,256,128]{3,2,1,0:T(8,128)(2,1)}, u32[]{:S(2)}, u32[]{:S(2)}) %collective-permute-start.15) | collective-permute-done | bytes 1048608 | tf_op jit(solution)/shard_map/ppermute | solution.py:85
  78.7 3.3 collective-permute-start.4
  82.0 7.8 %collective-permute-done.2.refs_4_ = bf16[2,256,768]{2,1,0:T(8,128)(2,1)} collective-permute-done((bf16[2,256,768]{2,1,0:T(8,128)(2,1)}, bf16[2,256,768]{2,1,0:T(8,128)(2,1)}, u32[]{:S(2)}, u32[]{:S(2)}) %collective-permute-start.2) | collective-permute-done | bytes 786464 | tf_op jit(solution)/shard_map/ppermute | solution.py:79
  92.6 41.6 %collective-permute-done.4.refs_6_ = bf16[2,256,768]{2,1,0:T(8,128)(2,1)} collective-permute-done((bf16[2,256,768]{2,1,0:T(8,128)(2,1)}, bf16[2,256,768]{2,1,0:T(8,128)(2,1)}, u32[]{:S(2)}, u32[]{:S(2)}) %collective-permute-start.4) | collective-permute-done | bytes 786464 | tf_op jit(solution)/shard_map/ppermute | solution.py:79
  134.3 126.7 %attention.1 = (bf16[2,256,768]{2,1,0:T(8,128)(2,1)}, bf16[2,256,768]{2,1,0:T(8,128)(2,1)}, bf16[2,256,768]{2,1,0:T(8,128)(2,1)}, bf16[2,256,768]{2,1,0:T(8,128)...) custom-call(s32[16,8]{1,0:T(8,128)} %copy.10.list_ref, ...), custom_call_target="tpu_custom_call" | custom-call | flops 77309411328 | bytes 33554432 | tf_op jit(solution)/shard_map/attention/pallas_call | solution.py:380
  261.9 5.2 %collective-permute-start.30 = (bf16[2,8,256,128]{3,2,1,0:T(8,128)(2,1)}, bf16[2,8,256,128]{3,2,1,0:T(8,128)(2,1)S(1)}, u32[]{:S(2)}, u32[]{:S(2)}) collective-permute-start(bf16[2,8,256,128]{3,2,1,0:T(8,128)(2,1)} %get-tuple-element.75), channel_id=1, source_target_pairs={{3,2},{7,6},{11,10},{15,14},{19,18},{23,22},{27,26},{31,30}} | collective-permute-start | bytes 3145736 | tf_op jit(solution)/shard_map/ppermute | solution.py:85
  269.5 20.0 %collective-permute-done.30 = bf16[2,8,256,128]{3,2,1,0:T(8,128)(2,1)S(1)} collective-permute-done((bf16[2,8,256,128]{3,2,1,0:T(8,128)(2,1)}, bf16[2,8,256,128]{3,2,1,0:T(8,128)(2,1)S(1)}, u32[]{:S(2)}, u32[]{:S(2)}) %collective-permute-start.30) | collective-permute-done | bytes 1048608 | tf_op jit(solution)/shard_map/ppermute | solution.py:85
  289.8 4.2 %collective-permute-start.31 = (bf16[2,8,256,128]{3,2,1,0:T(8,128)(2,1)S(1)}, bf16[2,8,256,128]{3,2,1,0:T(8,128)(2,1)S(1)}, u32[]{:S(2)}, u32[]{:S(2)}) collective-permute-start(bf16[2,8,256,128]{3,2,1,0:T(8,128)(2,1)S(1)} %add_convert_fusion.1), channel_id=1, source_target_pairs={{2,1},{6,5},{10,9},{14,13},{18,17},{22,21},{26,25},{30,29},{3,2},{... | collective-permute-start | bytes 3145736 | tf_op jit(solution)/shard_map/ppermute | solution.py:85
  295.7 19.4 %collective-permute-done.31 = bf16[2,8,256,128]{3,2,1,0:T(8,128)(2,1)S(1)} collective-permute-done((bf16[2,8,256,128]{3,2,1,0:T(8,128)(2,1)S(1)}, bf16[2,8,256,128]{3,2,1,0:T(8,128)(2,1)S(1)}, u32[]{:S(2)}, u32[]{:S(2)}) %collective-permute-start.31) | collective-permute-done | bytes 1048608 | tf_op jit(solution)/shard_map/ppermute | solution.py:85
  315.5 4.2 %collective-permute-start.32 = (bf16[2,8,256,128]{3,2,1,0:T(8,128)(2,1)S(1)}, bf16[2,8,256,128]{3,2,1,0:T(8,128)(2,1)S(1)}, u32[]{:S(2)}, u32[]{:S(2)}) collective-permute-start(bf16[2,8,256,128]{3,2,1,0:T(8,128)(2,1)S(1)} %add_convert_fusion), channel_id=1, source_target_pairs={{1,0},{5,4},{9,8},{13,12},{17,16},{21,20},{25,24},{29,28},{2,1},{6... | collective-permute-start | bytes 3145736 | tf_op jit(solution)/shard_map/ppermute | solution.py:85
  324.0 17.2 %collective-permute-done.21.refs_3_ = bf16[2,256,768]{2,1,0:T(8,128)(2,1)S(1)} collective-permute-done((bf16[2,256,768]{2,1,0:T(8,128)(2,1)S(1)}, bf16[2,256,768]{2,1,0:T(8,128)(2,1)S(1)}, u32[]{:S(2)}, u32[]{:S(2)}) %collective-permute-start.21) | collective-permute-done | bytes 786464 | tf_op jit(solution)/shard_map/ppermute | solution.py:79
  341.2 3.6 collective-permute-start.25
  345.9 2.9 split.1
  348.8 10.4 %collective-permute-done.22.refs_4_ = bf16[2,256,768]{2,1,0:T(8,128)(2,1)} collective-permute-done((bf16[2,256,768]{2,1,0:T(8,128)(2,1)}, bf16[2,256,768]{2,1,0:T(8,128)(2,1)}, u32[]{:S(2)}, u32[]{:S(2)}) %collective-permute-start.22) | collective-permute-done | bytes 786464 | tf_op jit(solution)/shard_map/ppermute | solution.py:79
  360.4 34.3 %collective-permute-done.24.refs_6_ = bf16[2,256,768]{2,1,0:T(8,128)(2,1)} collective-permute-done((bf16[2,256,768]{2,1,0:T(8,128)(2,1)}, bf16[2,256,768]{2,1,0:T(8,128)(2,1)}, u32[]{:S(2)}, u32[]{:S(2)}) %collective-permute-start.24) | collective-permute-done | bytes 786464 | tf_op jit(solution)/shard_map/ppermute | solution.py:79
  398.4 2.9 collective-permute-start.39
  401.3 6.3 %shard_map.96 = (bf16[256,6144]{1,0:T(8,128)(2,1)}, bf16[256,6144]{1,0:T(8,128)(2,1)}) custom-call(s32[2]{0:T(128)} %pad_add_fusion.refs_0_.where_ref, bf16[2,256,768]{2,1,0:T(8,128)(2,1)} %get-tuple-element.61.refs_1_, bf16[2,256,768]{2,1,0:T(8,128)(2,1)} %copy-done.5, bf16[2,256,768]{2,1,0:T(8,128)(2,1)} %copy-done.6, ...), custom_call_target="tpu_custom_call" | custom-call | bytes 12582912 | tf_op jit(solution)/shard_map/pallas_call | solution.py:104
  408.0 2.8 collective-permute-done.37.refs_6_
  411.5 3.0 shard_map.97
  (123 shorter events, 45.4 us)
Async XLA Ops:
  23.0 24.8 %collective-permute-start.17 = (bf16[2,8,256,128]{3,2,1,0:T(8,128)(2,1)}, bf16[2,8,256,128]{3,2,1,0:T(8,128)(2,1)S(1)}, u32[]{:S(2)}, u32[]{:S(2)}) collective-permute-start(bf16[2,8,256,128]{3,2,1,0:T(8,128)(2,1)} %shard_map.95.refs_9_), channel_id=1, source_target_pairs={{1,0},{5,4},{9,8},{13,12},{17,16},{21,20},{25,24},{29,28},{2,1},{6... | collective-permute-start | bytes 3145736 | tf_op jit(solution)/shard_map/ppermute | solution.py:85
  25.1 26.6 %collective-permute-start.14 = (bf16[2,8,256,128]{3,2,1,0:T(8,128)(2,1)}, bf16[2,8,256,128]{3,2,1,0:T(8,128)(2,1)}, u32[]{:S(2)}, u32[]{:S(2)}) collective-permute-start(bf16[2,8,256,128]{3,2,1,0:T(8,128)(2,1)} %shard_map.95.refs_9_), channel_id=1, source_target_pairs={{0,1},{4,5},{8,9},{12,13},{16,17},{20,21},{24,25},{28,29},{1,2},{5... | collective-permute-start | bytes 3145736 | tf_op jit(solution)/shard_map/ppermute | solution.py:85
  31.9 24.0 %collective-permute-start = (bf16[2,256,768]{2,1,0:T(8,128)(2,1)}, bf16[2,256,768]{2,1,0:T(8,128)(2,1)S(1)}, u32[]{:S(2)}, u32[]{:S(2)}) collective-permute-start(bf16[2,256,768]{2,1,0:T(8,128)(2,1)} %get-tuple-element.46), channel_id=1, source_target_pairs={{0,4},{4,0},{8,12},{12,8},{16,20},{20,16},{24,28},{28,24},{1,5},{5... | collective-permute-start | bytes 2359304 | tf_op jit(solution)/shard_map/ppermute | solution.py:79
  51.7 25.7 %collective-permute-start.15 = (bf16[2,8,256,128]{3,2,1,0:T(8,128)(2,1)}, bf16[2,8,256,128]{3,2,1,0:T(8,128)(2,1)}, u32[]{:S(2)}, u32[]{:S(2)}) collective-permute-start(bf16[2,8,256,128]{3,2,1,0:T(8,128)(2,1)} %collective-permute-done.14.refs_10_), channel_id=1, source_target_pairs={{1,2},{5,6},{9,10},{13,14},{17,18},{21,22},{25,26},{29,30},{2,3},{... | collective-permute-start | bytes 3145736 | tf_op jit(solution)/shard_map/ppermute | solution.py:85
  53.0 25.7 %collective-permute-start.1 = (bf16[2,256,768]{2,1,0:T(8,128)(2,1)}, bf16[2,256,768]{2,1,0:T(8,128)(2,1)}, u32[]{:S(2)}, u32[]{:S(2)}) collective-permute-start(bf16[2,256,768]{2,1,0:T(8,128)(2,1)} %get-tuple-element.47), channel_id=1, source_target_pairs={{0,8},{4,12},{8,0},{12,4},{16,24},{20,28},{24,16},{28,20},{1,9},{5... | collective-permute-start | bytes 2359304 | tf_op jit(solution)/shard_map/ppermute | solution.py:79
  54.3 35.5 %collective-permute-start.2 = (bf16[2,256,768]{2,1,0:T(8,128)(2,1)}, bf16[2,256,768]{2,1,0:T(8,128)(2,1)}, u32[]{:S(2)}, u32[]{:S(2)}) collective-permute-start(bf16[2,256,768]{2,1,0:T(8,128)(2,1)} %get-tuple-element.48), channel_id=1, source_target_pairs={{0,12},{4,8},{8,4},{12,0},{16,28},{20,24},{24,20},{28,16},{1,13},{... | collective-permute-start | bytes 2359304 | tf_op jit(solution)/shard_map/ppermute | solution.py:79
  55.9 36.1 %collective-permute-start.3 = (bf16[2,256,768]{2,1,0:T(8,128)(2,1)}, bf16[2,256,768]{2,1,0:T(8,128)(2,1)}, u32[]{:S(2)}, u32[]{:S(2)}) collective-permute-start(bf16[2,256,768]{2,1,0:T(8,128)(2,1)} %get-tuple-element.49), channel_id=1, source_target_pairs={{0,16},{4,20},{8,24},{12,28},{16,0},{20,4},{24,8},{28,12},{1,17},{... | collective-permute-start | bytes 2359304 | tf_op jit(solution)/shard_map/ppermute | solution.py:79
  57.2 77.1 %collective-permute-start.19 = (bf16[2,8,256,128]{3,2,1,0:T(8,128)(2,1)S(1)}, bf16[2,8,256,128]{3,2,1,0:T(8,128)(2,1)}, u32[]{:S(2)}, u32[]{:S(2)}) collective-permute-start(bf16[2,8,256,128]{3,2,1,0:T(8,128)(2,1)S(1)} %collective-permute-done.18.refs_14_), channel_id=1, source_target_pairs={{1,0},{5,4},{9,8},{13,12},{17,16},{21,20},{25,24},{29,28}} | collective-permute-start | bytes 3145736 | tf_op jit(solution)/shard_map/ppermute | solution.py:85
  77.4 56.8 %collective-permute-start.16 = (bf16[2,8,256,128]{3,2,1,0:T(8,128)(2,1)}, bf16[2,8,256,128]{3,2,1,0:T(8,128)(2,1)}, u32[]{:S(2)}, u32[]{:S(2)}) collective-permute-start(bf16[2,8,256,128]{3,2,1,0:T(8,128)(2,1)} %collective-permute-done.15.refs_11_), channel_id=1, source_target_pairs={{2,3},{6,7},{10,11},{14,15},{18,19},{22,23},{26,27},{30,31}} | collective-permute-start | bytes 3145736 | tf_op jit(solution)/shard_map/ppermute | solution.py:85
  78.7 55.5 %collective-permute-start.4 = (bf16[2,256,768]{2,1,0:T(8,128)(2,1)}, bf16[2,256,768]{2,1,0:T(8,128)(2,1)}, u32[]{:S(2)}, u32[]{:S(2)}) collective-permute-start(bf16[2,256,768]{2,1,0:T(8,128)(2,1)} %get-tuple-element.50), channel_id=1, source_target_pairs={{0,20},{4,16},{8,28},{12,24},{16,4},{20,0},{24,12},{28,8},{1,21},{... | collective-permute-start | bytes 2359304 | tf_op jit(solution)/shard_map/ppermute | solution.py:79
  89.8 44.4 %collective-permute-start.5 = (bf16[2,256,768]{2,1,0:T(8,128)(2,1)}, bf16[2,256,768]{2,1,0:T(8,128)(2,1)}, u32[]{:S(2)}, u32[]{:S(2)}) collective-permute-start(bf16[2,256,768]{2,1,0:T(8,128)(2,1)} %get-tuple-element.51), channel_id=1, source_target_pairs={{0,24},{4,28},{8,16},{12,20},{16,8},{20,12},{24,0},{28,4},{1,25},{... | collective-permute-start | bytes 2359304 | tf_op jit(solution)/shard_map/ppermute | solution.py:79
  92.0 42.3 %collective-permute-start.6 = (bf16[2,256,768]{2,1,0:T(8,128)(2,1)}, bf16[2,256,768]{2,1,0:T(8,128)(2,1)}, u32[]{:S(2)}, u32[]{:S(2)}) collective-permute-start(bf16[2,256,768]{2,1,0:T(8,128)(2,1)} %get-tuple-element.52), channel_id=1, source_target_pairs={{0,28},{4,24},{8,20},{12,16},{16,12},{20,8},{24,4},{28,0},{1,29},{... | collective-permute-start | bytes 2359304 | tf_op jit(solution)/shard_map/ppermute | solution.py:79
  261.9 27.6 %collective-permute-start.30 = (bf16[2,8,256,128]{3,2,1,0:T(8,128)(2,1)}, bf16[2,8,256,128]{3,2,1,0:T(8,128)(2,1)S(1)}, u32[]{:S(2)}, u32[]{:S(2)}) collective-permute-start(bf16[2,8,256,128]{3,2,1,0:T(8,128)(2,1)} %get-tuple-element.75), channel_id=1, source_target_pairs={{3,2},{7,6},{11,10},{15,14},{19,18},{23,22},{27,26},{31,30}} | collective-permute-start | bytes 3145736 | tf_op jit(solution)/shard_map/ppermute | solution.py:85
  268.7 25.3 %collective-permute-start.28 = (bf16[2,8,256,128]{3,2,1,0:T(8,128)(2,1)S(1)}, bf16[2,8,256,128]{3,2,1,0:T(8,128)(2,1)S(1)}, u32[]{:S(2)}, u32[]{:S(2)}) collective-permute-start(bf16[2,8,256,128]{3,2,1,0:T(8,128)(2,1)S(1)} %add_convert_fusion.3), channel_id=1, source_target_pairs={{0,1},{4,5},{8,9},{12,13},{16,17},{20,21},{24,25},{28,29},{1,2},{5... | collective-permute-start | bytes 3145736 | tf_op jit(solution)/shard_map/ppermute | solution.py:85
  289.8 25.4 %collective-permute-start.31 = (bf16[2,8,256,128]{3,2,1,0:T(8,128)(2,1)S(1)}, bf16[2,8,256,128]{3,2,1,0:T(8,128)(2,1)S(1)}, u32[]{:S(2)}, u32[]{:S(2)}) collective-permute-start(bf16[2,8,256,128]{3,2,1,0:T(8,128)(2,1)S(1)} %add_convert_fusion.1), channel_id=1, source_target_pairs={{2,1},{6,5},{10,9},{14,13},{18,17},{22,21},{26,25},{30,29},{3,2},{... | collective-permute-start | bytes 3145736 | tf_op jit(solution)/shard_map/ppermute | solution.py:85
  294.3 46.9 %collective-permute-start.29 = (bf16[2,8,256,128]{3,2,1,0:T(8,128)(2,1)S(1)}, bf16[2,8,256,128]{3,2,1,0:T(8,128)(2,1)S(1)}, u32[]{:S(2)}, u32[]{:S(2)}) collective-permute-start(bf16[2,8,256,128]{3,2,1,0:T(8,128)(2,1)S(1)} %add_convert_fusion.2), channel_id=1, source_target_pairs={{0,1},{4,5},{8,9},{12,13},{16,17},{20,21},{24,25},{28,29},{1,2},{5... | collective-permute-start | bytes 3145736 | tf_op jit(solution)/shard_map/ppermute | solution.py:85
  315.5 29.4 %collective-permute-start.32 = (bf16[2,8,256,128]{3,2,1,0:T(8,128)(2,1)S(1)}, bf16[2,8,256,128]{3,2,1,0:T(8,128)(2,1)S(1)}, u32[]{:S(2)}, u32[]{:S(2)}) collective-permute-start(bf16[2,8,256,128]{3,2,1,0:T(8,128)(2,1)S(1)} %add_convert_fusion), channel_id=1, source_target_pairs={{1,0},{5,4},{9,8},{13,12},{17,16},{21,20},{25,24},{29,28},{2,1},{6... | collective-permute-start | bytes 3145736 | tf_op jit(solution)/shard_map/ppermute | solution.py:85
  323.3 35.8 %collective-permute-start.22 = (bf16[2,256,768]{2,1,0:T(8,128)(2,1)}, bf16[2,256,768]{2,1,0:T(8,128)(2,1)}, u32[]{:S(2)}, u32[]{:S(2)}) collective-permute-start(bf16[2,256,768]{2,1,0:T(8,128)(2,1)} %get-tuple-element.64), channel_id=1, source_target_pairs={{0,12},{4,8},{8,4},{12,0},{16,28},{20,24},{24,20},{28,16},{1,13},{... | collective-permute-start | bytes 2359304 | tf_op jit(solution)/shard_map/ppermute | solution.py:79
  324.0 35.2 %collective-permute-start.23 = (bf16[2,256,768]{2,1,0:T(8,128)(2,1)}, bf16[2,256,768]{2,1,0:T(8,128)(2,1)}, u32[]{:S(2)}, u32[]{:S(2)}) collective-permute-start(bf16[2,256,768]{2,1,0:T(8,128)(2,1)} %get-tuple-element.65), channel_id=1, source_target_pairs={{0,16},{4,20},{8,24},{12,28},{16,0},{20,4},{24,8},{28,12},{1,17},{... | collective-permute-start | bytes 2359304 | tf_op jit(solution)/shard_map/ppermute | solution.py:79
  341.2 53.5 %collective-permute-start.24 = (bf16[2,256,768]{2,1,0:T(8,128)(2,1)}, bf16[2,256,768]{2,1,0:T(8,128)(2,1)}, u32[]{:S(2)}, u32[]{:S(2)}) collective-permute-start(bf16[2,256,768]{2,1,0:T(8,128)(2,1)} %get-tuple-element.66), channel_id=1, source_target_pairs={{0,20},{4,16},{8,28},{12,24},{16,4},{20,0},{24,12},{28,8},{1,21},{... | collective-permute-start | bytes 2359304 | tf_op jit(solution)/shard_map/ppermute | solution.py:79
  341.2 55.6 %collective-permute-start.25 = (bf16[2,256,768]{2,1,0:T(8,128)(2,1)}, bf16[2,256,768]{2,1,0:T(8,128)(2,1)}, u32[]{:S(2)}, u32[]{:S(2)}) collective-permute-start(bf16[2,256,768]{2,1,0:T(8,128)(2,1)} %get-tuple-element.67), channel_id=1, source_target_pairs={{0,24},{4,28},{8,16},{12,20},{16,8},{20,12},{24,0},{28,4},{1,25},{... | collective-permute-start | bytes 2359304 | tf_op jit(solution)/shard_map/ppermute | solution.py:79
  344.9 52.0 %collective-permute-start.26 = (bf16[2,256,768]{2,1,0:T(8,128)(2,1)}, bf16[2,256,768]{2,1,0:T(8,128)(2,1)}, u32[]{:S(2)}, u32[]{:S(2)}) collective-permute-start(bf16[2,256,768]{2,1,0:T(8,128)(2,1)} %get-tuple-element.68), channel_id=1, source_target_pairs={{0,28},{4,24},{8,20},{12,16},{16,12},{20,8},{24,4},{28,0},{1,29},{... | collective-permute-start | bytes 2359304 | tf_op jit(solution)/shard_map/ppermute | solution.py:79
  359.2 38.8 %collective-permute-start.33 = (bf16[2,256,128]{2,1,0:T(8,128)(2,1)}, bf16[2,256,128]{2,1,0:T(8,128)(2,1)S(1)}, u32[]{:S(2)}, u32[]{:S(2)}) collective-permute-start(bf16[2,256,128]{2,1,0:T(8,128)(2,1)} %get-tuple-element.79), channel_id=1, source_target_pairs={{0,4},{4,0},{8,12},{12,8},{16,20},{20,16},{24,28},{28,24},{1,5},{5... | collective-permute-start | bytes 393224 | tf_op jit(solution)/shard_map/ppermute | solution.py:79
  359.2 39.2 %collective-permute-start.34 = (bf16[2,256,128]{2,1,0:T(8,128)(2,1)}, bf16[2,256,128]{2,1,0:T(8,128)(2,1)S(1)}, u32[]{:S(2)}, u32[]{:S(2)}) collective-permute-start(bf16[2,256,128]{2,1,0:T(8,128)(2,1)} %get-tuple-element.80), channel_id=1, source_target_pairs={{0,8},{4,12},{8,0},{12,4},{16,24},{20,28},{24,16},{28,20},{1,9},{5... | collective-permute-start | bytes 393224 | tf_op jit(solution)/shard_map/ppermute | solution.py:79
  (43 other events, 713.7 us)
